TPU v7x, 32 devices: a whole 2x2x4 slice. The times are simulated.
32 devices in a mesh: ctx: 8 (over y, x, core), head: 4 (over z).
Axes of the slice: x: 2, y: 2, z: 4, core: 2. Of those that a mesh axis runs over, the one named last changes fastest.
Arguments:
- main_query: bfloat16 [1024, 73728], P('ctx', 'head'), as said below
- latents: bfloat16 [512, 576], P('ctx'), may hold values from -6 to 6, as said below
- idx_query: bfloat16 [1024, 8192], P('ctx'), as said below
- idx_weight: float32 [1024, 64], P('ctx'), may hold values from -9 to 9
- idx_keys: bfloat16 [512, 128], P('ctx'), may hold values from -6 to 6, as said below
- kl_cotangent: float32 [1024], P('ctx'), may hold values from 4 to 64
- query_start: int32 [1], replicated, may hold values from 256 to 511
- key_start: int32 [1], replicated, may hold values from 0 to 255
Outputs:
- grad_query: float32 [1024, 8192], P('ctx', 'head')
- grad_weight: float32 [1024, 64], P('ctx', 'head')
- grad_keys: float32 [512, 128], P(('ctx', 'head'))
Inputs may be any that keep to these rules, and one draw needn't show every extreme that they name: `latents`: saved latent keys of order one. `idx_keys`: indexer keys of order one. `main_query`: attention queries; a few rows may be large. `idx_query`: indexer queries; a few rows may be large.
All inputs are finite; a program needn't handle non-finite values.
Results may differ from a plain program's by a relative error of at most 0.02.
Values may be sent and summed in bfloat16 or wider, within the bound.
A program may use at most 128 MiB of HBM per device.

v0:
```python
import jax
import jax.numpy as jnp
from jax import lax
from jax.sharding import PartitionSpec as P

NEGATIVE = -1e30
MAIN_SCALE = 192.0 ** (-0.5)


def merged(value, axis, join):
    pieces = jax.tree.map(lambda part: lax.all_gather(part, axis), value)
    head = jax.tree.map(lambda part: part[0], pieces)
    tail = jax.tree.map(lambda part: part[1:], pieces)
    running, _ = lax.scan(lambda running, section: (join(running, section), None), head, tail)
    return running


def group_size(heads, per_head, limit):
    group = 1
    while group * 2 <= heads and heads % (group * 2) == 0 and (group * 2 * per_head <= limit):
        group = group * 2
    return group


def head_totals(queries, keys, visible):
    query_rows, heads, width = queries.shape
    key_count = keys.shape[0]
    group = group_size(heads, query_rows, 1024)

    def add_group(group_index, totals):
        block = lax.dynamic_slice_in_dim(queries, group_index * group, group, 1).reshape(
            query_rows * group, width
        )
        scores = lax.dot_general(
            block, keys, (((1,), (1,)), ((), ())), preferred_element_type=jnp.float32
        )
        scores = scores.reshape(query_rows, group, key_count) * MAIN_SCALE
        scores = jnp.where(visible[:, None, :], scores, NEGATIVE)
        largest = jnp.max(scores, axis=-1, keepdims=True)
        weights = jnp.where(visible[:, None, :], jnp.exp(scores - largest), 0.0)
        weights = weights / jnp.sum(weights, axis=-1, keepdims=True)
        return totals + jnp.sum(weights, axis=1)

    start_totals = jnp.zeros((query_rows, key_count), jnp.float32)
    return lax.fori_loop(0, heads // group, add_group, start_totals)


def index_scores(queries, keys, weights):
    query_rows, heads, head_dim = queries.shape
    key_count = keys.shape[0]
    group = group_size(heads, query_rows * key_count, 2**21)
    scale = head_dim ** (-0.5)

    def add_group(group_index, logits):
        block = lax.dynamic_slice_in_dim(queries, group_index * group, group, 1).reshape(
            query_rows * group, head_dim
        )
        inner = lax.dot_general(
            block, keys, (((1,), (1,)), ((), ())), preferred_element_type=jnp.float32
        )
        inner = inner.reshape(query_rows, group, key_count) * scale
        gains = lax.dynamic_slice_in_dim(weights, group_index * group, group, 1)
        return logits + jnp.sum(gains[:, :, None] * jnp.maximum(inner, 0.0), axis=1)

    start_logits = jnp.zeros((query_rows, key_count), jnp.float32)
    return lax.fori_loop(0, heads // group, add_group, start_logits)


def index_grads(queries, keys, weights, upstream):
    query_rows, heads, head_dim = queries.shape
    key_count = keys.shape[0]
    group = group_size(heads, query_rows * key_count, 2**21)
    scale = head_dim ** (-0.5)

    def add_group(group_index, carry):
        query_grad, weight_grad, key_grad = carry
        block = lax.dynamic_slice_in_dim(queries, group_index * group, group, 1).reshape(
            query_rows * group, head_dim
        )
        inner = lax.dot_general(
            block, keys, (((1,), (1,)), ((), ())), preferred_element_type=jnp.float32
        )
        inner = inner.reshape(query_rows, group, key_count) * scale
        gains = lax.dynamic_slice_in_dim(weights, group_index * group, group, 1)
        grad_inner = jnp.where(inner > 0.0, upstream[:, None, :] * gains[:, :, None], 0.0).astype(
            jnp.bfloat16
        )
        part_weight = jnp.sum(upstream[:, None, :] * jnp.maximum(inner, 0.0), axis=-1)
        grad_flat = grad_inner.reshape(query_rows * group, key_count)
        part_query = (
            jnp.dot(grad_flat, keys, preferred_element_type=jnp.float32).reshape(
                query_rows, group, head_dim
            )
            * scale
        )
        part_key = (
            lax.dot_general(
                grad_flat, block, (((0,), (0,)), ((), ())), preferred_element_type=jnp.float32
            )
            * scale
        )
        query_grad = lax.dynamic_update_slice_in_dim(query_grad, part_query, group_index * group, 1)
        weight_grad = lax.dynamic_update_slice_in_dim(
            weight_grad, part_weight, group_index * group, 1
        )
        return (query_grad, weight_grad, key_grad + part_key)

    start_carry = (
        jnp.zeros((query_rows, heads, head_dim), jnp.float32),
        jnp.zeros((query_rows, heads), jnp.float32),
        jnp.zeros((key_count, head_dim), jnp.float32),
    )
    return lax.fori_loop(0, heads // group, add_group, start_carry)


def regroup(values, ctx_count, head_count):
    total_rows = values.shape[0]
    per_block = total_rows // (ctx_count * head_count)
    shaped = values.reshape(ctx_count, head_count, per_block, values.shape[1])
    return shaped.transpose(1, 0, 2, 3).reshape(total_rows, values.shape[1])


def merge_stats(first, second):
    largest = jnp.maximum(first[0], second[0])
    return (
        largest,
        first[1] * jnp.exp(first[0] - largest) + second[1] * jnp.exp(second[0] - largest),
    )


def shards(
    main_query, latents, idx_query, idx_weight, idx_keys, kl_cotangent, query_start, key_start
):
    query_rows = main_query.shape[0]
    width = latents.shape[1]
    heads_here = main_query.shape[1] // width
    idx_heads = idx_weight.shape[1]
    idx_dim = idx_keys.shape[1]
    ctx_count = lax.axis_size("ctx")
    head_count = lax.axis_size("head")
    head_index = lax.axis_index("head")
    slab_latents, slab_index_keys = (
        lax.all_gather(latents, "ctx", axis=0, tiled=True),
        lax.all_gather(idx_keys, "ctx", axis=0, tiled=True),
    )
    key_count = slab_latents.shape[0]
    key_order = jnp.arange(key_count, dtype=jnp.int32)[:, None]
    slab_latents = regroup(slab_latents, ctx_count, head_count)
    slab_index_keys = regroup(slab_index_keys, ctx_count, head_count)
    key_order = regroup(key_order, ctx_count, head_count)
    key_position = key_start[0] + key_order[:, 0]
    query_position = (
        query_start[0]
        + lax.axis_index("ctx") * query_rows
        + jnp.arange(query_rows, dtype=jnp.int32)
    )
    visible = key_position[None, :] <= query_position[:, None]
    target = head_totals(main_query.reshape(query_rows, heads_here, width), slab_latents, visible)
    all_heads = heads_here * head_count
    block_keys = key_count // head_count
    target_block = lax.psum_scatter(target, "head", scatter_dimension=1, tiled=True) / all_heads
    keys_block = lax.dynamic_slice_in_dim(slab_index_keys, head_index * block_keys, block_keys, 0)
    visible_block = lax.dynamic_slice_in_dim(visible, head_index * block_keys, block_keys, 1)
    queries_index = idx_query.reshape(query_rows, idx_heads, idx_dim)
    logits = index_scores(queries_index, keys_block, idx_weight)
    logits = jnp.where(visible_block, logits, NEGATIVE)
    largest = jnp.max(logits, axis=-1, keepdims=True)
    total_exp = jnp.sum(
        jnp.where(visible_block, jnp.exp(logits - largest), 0.0), axis=-1, keepdims=True
    )
    largest, total_exp = merged((largest, total_exp), "head", merge_stats)
    chance = jnp.where(visible_block, jnp.exp(logits - largest) / total_exp, 0.0)
    upstream = kl_cotangent[:, None] * (chance - target_block)
    query_grad, weight_grad, key_grad = index_grads(queries_index, keys_block, idx_weight, upstream)
    grad_query, grad_weight = (
        lax.psum_scatter(
            query_grad.reshape(query_rows, idx_heads * idx_dim),
            "head",
            scatter_dimension=1,
            tiled=True,
        ),
        lax.psum_scatter(weight_grad, "head", scatter_dimension=1, tiled=True),
    )
    grad_keys = lax.psum_scatter(
        key_grad.astype(jnp.bfloat16), "ctx", scatter_dimension=0, tiled=True
    ).astype(jnp.float32)
    return (grad_query, grad_weight, grad_keys)


def solution(mesh):
    placed = (
        P("ctx", "head"),
        P("ctx", None),
        P("ctx", None),
        P("ctx", None),
        P("ctx", None),
        P("ctx"),
        P(),
        P(),
    )
    return jax.shard_map(
        shards,
        mesh=mesh,
        in_specs=placed,
        out_specs=(P("ctx", "head"), P("ctx", "head"), P(("ctx", "head"), None)),
        check_vma=False,
    )
```

profile of v0, /device:TPU:0, one launch (start us, length us, event | category | flops | bytes accessed | tf_op | source)
XLA Modules:
  0.0 257.5 jit_solution(1309100383372391707)
XLA Ops:
  7.2 0.0 reduce-scatter.7.cloned.1.call-start
  7.9 0.1 add.119
  8.6 0.0 copy-start.3
  8.6 6.7 %copy.49 = bf16[128,18432]{0,1:T(8,128)(2,1)} copy(bf16[128,18432]{1,0:T(8,128)(2,1)} %param.12) | data formatting | bytes 9437184 | tf_op args[0]
  15.3 11.6 %all_gather.15 = bf16[512,576]{1,0:T(8,128)(2,1)S(1)} all-gather(bf16[64,576]{1,0:T(8,128)(2,1)S(1)} %copy-done.3), channel_id=1, replica_groups=mesh['ctx'=8,'head'=4] {'ctx'}, dimensions={0}, use_global_device_ids=true | all-gather | bytes 663552 | tf_op jit(solution)/shard_map/all_gather | solution.py:143
  26.9 0.1 copy.50
  26.9 0.2 copy.51
  27.2 32.0 %while.8 = (s32[]{:T(128)}, f32[128,512]{1,0:T(8,128)S(1)}, bf16[128,32,576]{0,2,1:T(8,128)(2,1)}, bf16[512,576]{0,1:T(8,128)(2,1)S(1)}, s32[128]{0:T(128)S(1)},...) while((s32[]{:T(128)}, f32[128,512]{1,0:T(8,128)S(1)}, ...), condition=%wide.region_9.10_spmd.clone, body=%wide.region_5.9_spmd.clone.sunk | while | flops 1213338112 | bytes 9112229 | solution.py:45
  27.2 0.1 broadcast_compare_fusion.2
  27.3 4.2 %fusion.84 = f32[128,8,512]{2,0,1:T(8,128)} fusion(pred[128,512]{1,0:T(8,128)(4,1)S(1)} %broadcast_compare_fusion.2, bf16[128,32,576]{0,2,1:T(8,128)(2,1)} %get-tuple-element.345, s32[]{:T(128)S(6)} %select_n.92, bf16[512,576]{0,1:T(8,128)(2,1)S(1)} %get-tuple-element.346), kind=kOutput, calls=%fused_computation.8.clone.1 | convolution fusion | flops 606080000 | bytes 3997700 | tf_op jit(solution)/shard_map/while/body/eval_jaxpr/div | solution.py:41
  31.5 3.6 %divide_reduce_fusion.2 = f32[128,512]{1,0:T(8,128)S(1)} fusion(f32[128,8,512]{2,0,1:T(8,128)} %fusion.84, pred[128,512]{1,0:T(8,128)(4,1)S(1)} %broadcast_compare_fusion.2, bf16[512,576]{0,1:T(8,128)(2,1)S(1)} %get-tuple-element.346, bf16[128,32,576]{0,2,1:T(8,128)(2,1)} %get-tuple-element.345, s32[]{:T(128)S(6)} %select_n.92), kind=kOutput, calls=%fused_computation.12.clone.1 | convolution fusion | flops 607061504 | bytes 4259844 | tf_op jit(solution)/shard_map/while/body/eval_jaxpr/sub | solution.py:40
  35.1 0.1 select_add_fusion.2
  35.2 0.1 broadcast_compare_fusion.2
  35.3 4.2 %fusion.84 = f32[128,8,512]{2,0,1:T(8,128)} fusion(pred[128,512]{1,0:T(8,128)(4,1)S(1)} %broadcast_compare_fusion.2, bf16[128,32,576]{0,2,1:T(8,128)(2,1)} %get-tuple-element.345, s32[]{:T(128)S(6)} %select_n.92, bf16[512,576]{0,1:T(8,128)(2,1)S(1)} %get-tuple-element.346), kind=kOutput, calls=%fused_computation.8.clone.1 | convolution fusion | flops 606080000 | bytes 3997700 | tf_op jit(solution)/shard_map/while/body/eval_jaxpr/div | solution.py:41
  39.5 3.6 %divide_reduce_fusion.2 = f32[128,512]{1,0:T(8,128)S(1)} fusion(f32[128,8,512]{2,0,1:T(8,128)} %fusion.84, pred[128,512]{1,0:T(8,128)(4,1)S(1)} %broadcast_compare_fusion.2, bf16[512,576]{0,1:T(8,128)(2,1)S(1)} %get-tuple-element.346, bf16[128,32,576]{0,2,1:T(8,128)(2,1)} %get-tuple-element.345, s32[]{:T(128)S(6)} %select_n.92), kind=kOutput, calls=%fused_computation.12.clone.1 | convolution fusion | flops 607061504 | bytes 4259844 | tf_op jit(solution)/shard_map/while/body/eval_jaxpr/sub | solution.py:40
  43.1 0.1 select_add_fusion.2
  43.2 0.1 broadcast_compare_fusion.2
  43.3 4.2 %fusion.84 = f32[128,8,512]{2,0,1:T(8,128)} fusion(pred[128,512]{1,0:T(8,128)(4,1)S(1)} %broadcast_compare_fusion.2, bf16[128,32,576]{0,2,1:T(8,128)(2,1)} %get-tuple-element.345, s32[]{:T(128)S(6)} %select_n.92, bf16[512,576]{0,1:T(8,128)(2,1)S(1)} %get-tuple-element.346), kind=kOutput, calls=%fused_computation.8.clone.1 | convolution fusion | flops 606080000 | bytes 3997700 | tf_op jit(solution)/shard_map/while/body/eval_jaxpr/div | solution.py:41
  47.5 3.6 %divide_reduce_fusion.2 = f32[128,512]{1,0:T(8,128)S(1)} fusion(f32[128,8,512]{2,0,1:T(8,128)} %fusion.84, pred[128,512]{1,0:T(8,128)(4,1)S(1)} %broadcast_compare_fusion.2, bf16[512,576]{0,1:T(8,128)(2,1)S(1)} %get-tuple-element.346, bf16[128,32,576]{0,2,1:T(8,128)(2,1)} %get-tuple-element.345, s32[]{:T(128)S(6)} %select_n.92), kind=kOutput, calls=%fused_computation.12.clone.1 | convolution fusion | flops 607061504 | bytes 4259844 | tf_op jit(solution)/shard_map/while/body/eval_jaxpr/sub | solution.py:40
  51.1 0.1 select_add_fusion.2
  51.2 0.1 broadcast_compare_fusion.2
  51.3 4.2 %fusion.84 = f32[128,8,512]{2,0,1:T(8,128)} fusion(pred[128,512]{1,0:T(8,128)(4,1)S(1)} %broadcast_compare_fusion.2, bf16[128,32,576]{0,2,1:T(8,128)(2,1)} %get-tuple-element.345, s32[]{:T(128)S(6)} %select_n.92, bf16[512,576]{0,1:T(8,128)(2,1)S(1)} %get-tuple-element.346), kind=kOutput, calls=%fused_computation.8.clone.1 | convolution fusion | flops 606080000 | bytes 3997700 | tf_op jit(solution)/shard_map/while/body/eval_jaxpr/div | solution.py:41
  55.5 3.6 %divide_reduce_fusion.2 = f32[128,512]{1,0:T(8,128)S(1)} fusion(f32[128,8,512]{2,0,1:T(8,128)} %fusion.84, pred[128,512]{1,0:T(8,128)(4,1)S(1)} %broadcast_compare_fusion.2, bf16[512,576]{0,1:T(8,128)(2,1)S(1)} %get-tuple-element.346, bf16[128,32,576]{0,2,1:T(8,128)(2,1)} %get-tuple-element.345, s32[]{:T(128)S(6)} %select_n.92), kind=kOutput, calls=%fused_computation.12.clone.1 | convolution fusion | flops 607061504 | bytes 4259844 | tf_op jit(solution)/shard_map/while/body/eval_jaxpr/sub | solution.py:40
  59.1 0.1 select_add_fusion.2
  59.2 0.0 copy-start.2
  59.2 0.7 copy-done.2
  59.9 0.0 reduce-scatter.7.cloned.1.call-update
  59.9 0.0 reduce-scatter.11.cloned.1.call-start
  60.0 2.9 %reshape.105 = bf16[8192,128]{1,0:T(8,128)(2,1)S(1)} reshape(bf16[128,8192]{1,0:T(8,128)(2,1)} %param.14) | data formatting | bytes 4194304 | tf_op jit(solution)/shard_map/while/body/eval_jaxpr/reshape | solution.py:77
  62.9 9.2 %all_gather.12 = bf16[512,128]{1,0:T(8,128)(2,1)S(1)} all-gather(bf16[64,128]{1,0:T(8,128)(2,1)S(1)} %copy-done.5), channel_id=1, replica_groups=mesh['ctx'=8,'head'=4] {'ctx'}, dimensions={0}, use_global_device_ids=true | all-gather | bytes 147456 | tf_op jit(solution)/shard_map/all_gather | solution.py:144
  72.1 0.1 dynamic-slice
  72.2 0.7 convolution_multiply_fusion
  72.9 1.9 copy-done
  74.8 2.3 maximum_bitcast_fusion
  77.1 5.6 %copy.48 = f32[8192,128]{1,0:T(8,128)} copy(f32[8192,128]{0,1:T(8,128)} %maximum_bitcast_fusion) | data formatting | bytes 8388608 | tf_op jit(solution)/shard_map/while/body/eval_jaxpr/max | solution.py:63
  82.7 0.1 copy.47
  82.8 2.9 %multiply_reduce_fusion.1 = f32[128,128]{1,0:T(8,128)S(1)} fusion(f32[128,64]{1,0:T(8,128)S(1)} %copy.47, f32[8192,128]{1,0:T(8,128)} %copy.48), kind=kLoop, calls=%fused_computation.34 | loop fusion | flops 2080768 | bytes 4292608 | tf_op jit(solution)/shard_map/while/body/eval_jaxpr/reduce_sum | solution.py:63
  85.7 0.2 fusion.59
  85.8 0.2 fusion.58
  86.0 11.1 %all-gather.3 = f32[4,1,128]{2,1,0:T(1,128)S(1)} all-gather(f32[1,1,128]{2,1,0:T(1,128)S(1)} %bitcast.100), channel_id=3, replica_groups=mesh['ctx'=8,'head'=4] {'head'}, dimensions={0}, use_global_device_ids=true | all-gather | bytes 2560 | tf_op jit(solution)/shard_map/all_gather | solution.py:11
  97.2 7.6 %all-gather.2 = f32[4,1,128]{2,1,0:T(1,128)S(1)} all-gather(f32[1,1,128]{2,1,0:T(1,128)S(1)} %bitcast.99), channel_id=2, replica_groups=mesh['ctx'=8,'head'=4] {'head'}, dimensions={0}, use_global_device_ids=true | all-gather | bytes 2560 | tf_op jit(solution)/shard_map/all_gather | solution.py:11
  104.7 0.1 mul.116
  104.8 0.1 while.7
  104.9 0.0 reduce-scatter.7.cloned.1.call-done
  105.0 1.0 fusion.57
  105.9 2.2 mul.114
  108.2 5.6 %copy.53 = f32[8192,128]{0,1:T(8,128)} copy(f32[8192,128]{1,0:T(8,128)} %bitcast.88) | data formatting | bytes 8388608 | tf_op jit(solution)/shard_map/while/body/eval_jaxpr/mul | solution.py:85
  113.8 4.4 %multiply_reduce_fusion = (f32[8192]{0:T(1024)S(1)}, bf16[8192,128]{0,1:T(8,128)(2,1)S(1)}) fusion(f32[8192,128]{0,1:T(8,128)} %copy.53, f32[128,8192]{1,0:T(8,128)} %copy-done, f32[8192]{0:T(1024)S(1)} %mul.116), kind=kLoop, calls=%fused_computation.32 | loop fusion | flops 7331840 | bytes 10551296 | tf_op jit(solution)/shard_map/while/body/eval_jaxpr/reduce_sum | solution.py:88
  118.3 1.3 copy-done.1
  119.6 1.3 fusion.55
  121.0 0.0 reduce-scatter.11.cloned.1.call-update
  121.0 0.0 reduce-scatter.13.cloned.1.call-start
  121.1 3.2 %copy.54 = bf16[8192,128]{1,0:T(8,128)(2,1)S(1)} copy(bf16[8192,128]{0,1:T(8,128)(2,1)} %copy-done.1) | data formatting | bytes 4194304 | tf_op jit(solution)/shard_map/while/body/eval_jaxpr/convert_element_type | solution.py:85
  124.3 0.1 reduce_sum.60
  124.4 0.7 copy.59
  125.1 0.0 reduce-scatter.13.cloned.1.call-update
  125.1 0.0 reduce-scatter.9.cloned.1.call-start
  125.1 3.8 %convolution_multiply_fusion.1 = f32[128,64,128]{0,2,1:T(8,128)} fusion(bf16[128,64,128]{2,1,0:T(8,128)(2,1)S(1)} %bitcast.89, bf16[512,128]{1,0:T(8,128)(2,1)S(1)} %bitcast.95, s32[]{:T(128)S(6)} %select_n.50), kind=kOutput, calls=%fused_computation.36 | convolution fusion | flops 269484032 | bytes 6324228 | tf_op jit(solution)/shard_map/while/body/eval_jaxpr/dot_general | solution.py:91
  128.9 5.6 %copy.56 = f32[128,8192]{1,0:T(8,128)} copy(f32[128,8192]{0,1:T(8,128)} %bitcast.87) | data formatting | bytes 8388608 | tf_op jit(solution)/shard_map/reshape | solution.py:177
  134.5 0.0 reduce-scatter.9.cloned.1.call-update
  134.6 16.7 %reduce-scatter.11.cloned.1.call-done = bf16[16,128]{1,0:T(8,128)(2,1)} async-done(((bf16[128,128]{1,0:T(8,128)(2,1)}), bf16[16,128]{1,0:T(8,128)(2,1)}) %reduce-scatter.11.cloned.1.call-update) | async-done | bytes 4112 | tf_op jit(solution)/shard_map/reduce_scatter | solution.py:184
  151.2 1.3 convert_element_type.13
  152.5 20.8 %reduce-scatter.13.cloned.1.call-done = f32[16,128]{1,0:T(8,128)} async-done(((f32[64,128]{1,0:T(8,128)}), f32[16,128]{1,0:T(8,128)}) %reduce-scatter.13.cloned.1.call-update) | async-done | bytes 8208
  173.3 77.7 %reduce-scatter.9.cloned.1.call-done = f32[128,2048]{1,0:T(8,128)} async-done(((f32[128,8192]{1,0:T(8,128)}), f32[128,2048]{1,0:T(8,128)}) %reduce-scatter.9.cloned.1.call-update) | async-done | bytes 1048592 | tf_op jit(solution)/shard_map/reduce_scatter | solution.py:176
  (20 shorter events, 0.1 us)
Async XLA Ops:
  7.2 97.8 %reduce-scatter.7.cloned.1.call-start = ((), (), s32[]{:S(2)}) async-start(), calls=%async_computation.4 | async-start | bytes 327680 | tf_op jit(solution)/shard_map/reduce_scatter | solution.py:161
  8.6 6.7 %copy-start.3 = (bf16[64,576]{1,0:T(8,128)(2,1)S(1)}, bf16[64,576]{1,0:T(8,128)(2,1)}, u32[]{:S(2)}) copy-start(bf16[64,576]{1,0:T(8,128)(2,1)} %param.13) | copy-start | bytes 221188
  59.2 0.7 copy-start.2
  59.9 91.3 %reduce-scatter.11.cloned.1.call-start = ((), (), s32[]{:S(2)}) async-start(), calls=%async_computation.6 | async-start | bytes 36864 | tf_op jit(solution)/shard_map/reduce_scatter | solution.py:184
  60.0 2.9 %copy-start.5 = (bf16[64,128]{1,0:T(8,128)(2,1)S(1)}, bf16[64,128]{1,0:T(8,128)(2,1)}, u32[]{:S(2)}) copy-start(bf16[64,128]{1,0:T(8,128)(2,1)} %param.16) | copy-start | bytes 49156
  72.9 1.9 copy-start
  77.1 5.6 %copy-start.4 = (f32[128,64]{0,1:T(8,128)S(1)}, f32[128,64]{0,1:T(8,128)}, u32[]{:S(2)}) copy-start(f32[128,64]{0,1:T(8,128)} %param.15) | copy-start | bytes 98308
  82.8 22.2 %copy-start.6 = (f32[128]{0:T(128)S(1)}, f32[128]{0:T(128)}, u32[]{:S(2)}) copy-start(f32[128]{0:T(128)} %param.17) | copy-start | bytes 1540
  118.3 1.4 copy-start.1
  121.0 52.3 %reduce-scatter.13.cloned.1.call-start = ((), (), s32[]{:S(2)}) async-start(), calls=%async_computation.7 | async-start | bytes 40960
  125.1 125.9 %reduce-scatter.9.cloned.1.call-start = ((), (), s32[]{:S(2)}) async-start(), calls=%async_computation.5 | async-start | bytes 5242880 | tf_op jit(solution)/shard_map/reduce_scatter | solution.py:176
Sparse Core Ops, SparseCore 0:
  60.0 20.2 reduce-scatter.6
  121.1 30.0 reduce-scatter.10
  154.1 19.1 reduce-scatter.12
  176.0 74.9 reduce-scatter.8
where the time goes:
time: 258 us; the launch traced here: 257 us
  waiting for transfers between devices  115 us (45%)
  blocking collectives  39.5 us (15%)
  local copies, waits for them, and re-layouts  37.3 us (14%)
  matrix products  36.8 us (14%)
  between operations  15.3 us (6%)
  other arithmetic  13.1 us (5%)
    reduce_scatter x1, waiting for transfers between devices, shards(): lax.psum_scatter(query_grad.reshape(query_rows, idx_heads * idx_dim), 'he...  77.7 us
    unnamed x5, waiting for transfers between devices  20.8 us
    all_gather x2, blocking collectives, merged(): pieces = jax.tree.map(lambda part: lax.all_gather(part, axis), value)  18.7 us
    div x4, matrix products, add_group(): weights = weights / jnp.sum(weights, axis=-1, keepdims=True)  16.8 us
    reduce_scatter x1, waiting for transfers between devices, shards(): lax.psum_scatter(key_grad.astype(jnp.bfloat16), 'ctx', scatter_dimension=...  16.7 us
    sub x4, matrix products, add_group(): weights = jnp.where(visible[:, None, :], jnp.exp(scores - largest), 0.0)  14.3 us
    unnamed x18, local copies, waits for them, and re-layouts  11.7 us
    all_gather x1, blocking collectives, shards(): lax.all_gather(latents, 'ctx', axis=0, tiled=True)  11.6 us
  transfers between devices with their start and end apart: 4, of which 3 were waited for; matrix products, arithmetic and copies ran while one was open for 12% of the time, Pallas kernels for 0%

commit v1 on v0

v1 whole, which is shorter than its diff:
```python
import functools
import math

import jax
import jax.numpy as jnp
from jax import lax
from jax.experimental import pallas as pl
from jax.experimental.pallas import tpu as pltpu
from jax.sharding import PartitionSpec as P

NEGATIVE = -1e30
LOG2E = math.log2(math.e)
MAIN_SCALE = 192.0 ** (-0.5)
MESH = pl.DeviceIdType.MESH
NT = (((1,), (1,)), ((), ()))


def kernel(
    n, hc, qs_ref, ks_ref, main_ref, lat_ref, iq_ref, w_ref, ik_ref, cot_ref,
    gq_ref, gw_ref, gk_ref,
    q_buf, iql, iqg, lat_all, ik_all, k_even, k_odd, t_send, t_recv, u_send, u_all, w_all, gains_all, gw_wide, dk, dk_send, dk_recv, z_send, z_recv,
    q_sem, i_sem, lat_s, lat_r, lat_f, ik_s, ik_r, ik_f, t_s, t_r, u_s, u_r, d_s, d_r, z_s, z_r,
):
    me = lax.axis_index("ctx")
    h = lax.axis_index("head")
    pairs, rows, pair_width = q_buf.shape
    width = pair_width // 2
    block, key_width = lat_ref.shape[0], k_even.shape[1]
    keys = n * block
    heads = w_ref.shape[0]
    dim = ik_ref.shape[1]
    part = rows // hc
    own_heads = heads // hc
    scale = dim ** (-0.5)
    shift = pair_width - key_width

    loads = [
        pltpu.make_async_copy(iq_ref.at[pl.ds(pl.multiple_of(h * part, part), part), :], iql, i_sem.at[0]),
        pltpu.make_async_copy(
            iq_ref.at[:, pl.ds(pl.multiple_of(h * own_heads * dim, own_heads * dim), own_heads * dim)], iqg, i_sem.at[1]
        ),
    ]
    q_loads = [
        pltpu.make_async_copy(main_ref.at[:, pl.ds(p * pair_width, pair_width)], q_buf.at[p], q_sem.at[p])
        for p in range(pairs)
    ]
    for copy in loads + q_loads:
        copy.start()

    barrier = pltpu.get_barrier_semaphore()
    for t in range(1, n):
        pl.semaphore_signal(barrier, inc=1, device_id={"ctx": lax.rem(me + t, n)}, device_id_type=MESH)
    for k in range(1, hc):
        pl.semaphore_signal(barrier, inc=1, device_id={"head": lax.rem(h + k, hc)}, device_id_type=MESH)
    pl.semaphore_wait(barrier, n - 1 + hc - 1)

    parity = lax.rem(me, 2)
    partner = me + 1 - 2 * parity
    if hc == 4:
        others = [hc - 1 - h, lax.rem(h + 2, hc), h + 1 - 2 * lax.rem(h, 2)]
        sources = others
    else:
        others = [lax.rem(h + k, hc) for k in range(1, hc)]
        sources = [lax.rem(h - k + hc, hc) for k in range(1, hc)]

    def push(src, dst, at, to, send, recv):
        return pltpu.make_async_remote_copy(
            src_ref=src, dst_ref=dst.at[at], send_sem=send, recv_sem=recv.at[at],
            device_id={"ctx": to}, device_id_type=MESH,
        )

    def spread(src, dst, send, recv, forward):
        direct, relays, arrivals = [], [], []
        own = push(src, dst, me, partner, forward.at[0], recv)
        if n == 8:
            beside = me + 2 - 4 * lax.rem(me // 2, 2)
            across = me + 4 - 8 * (me // 4)
            far = beside + across - me
            source = beside + parity * (across - beside)
            target = across + parity * (beside - across)
            direct = [push(src, dst, me, source, send.at[1], recv), push(src, dst, me, target, send.at[2], recv)]
            relays = [
                [push(dst.at[source], dst, source, target, send.at[3], recv),
                 push(dst.at[source], dst, source, partner, forward.at[1], recv)],
                [push(dst.at[target], dst, target, partner, forward.at[2], recv)],
                [push(dst.at[far], dst, far, partner, forward.at[3], recv)],
            ]
        else:
            for t in range(1, n // 2):
                at = lax.rem(me - 2 * t + n, n)
                direct.append(push(src, dst, me, lax.rem(me + 2 * t, n), send.at[t], recv))
                relays.append([push(dst.at[at], dst, at, partner, forward.at[t], recv)])
        for t in range(n // 2):
            at = lax.rem(partner - 2 * t + n, n)
            arrivals.append(push(src, dst, at, partner, forward.at[t], recv))
        return direct + [own], relays, arrivals

    def relay(steps):
        for step in steps:
            step[0].wait_recv()
            for copy in step:
                copy.start()

    ik_direct, ik_relays, ik_arrivals = spread(ik_ref, ik_all, ik_s, ik_r, ik_f)
    lat_direct, lat_relays, lat_arrivals = spread(lat_ref, lat_all, lat_s, lat_r, lat_f)
    for copy in ik_direct + lat_direct:
        copy.start()
    ik_all[me] = ik_ref[...]
    lat_all[me] = lat_ref[...]
    w_t = jnp.transpose(w_ref[...])
    w_all[...] = w_t
    gains_all[...] = jnp.transpose(w_ref[pl.ds(pl.multiple_of(h * own_heads, own_heads), own_heads), :])
    relay(ik_relays)
    for copy in ik_arrivals:
        copy.wait_recv()
    for copy in loads:
        copy.wait()

    key_at = ks_ref[0] + lax.broadcasted_iota(jnp.int32, (part, keys), 1)
    row_at = qs_ref[0] + me * rows + lax.broadcasted_iota(jnp.int32, (part, keys), 0)

    def bias_of(chunk):
        return jnp.where(key_at <= row_at + chunk * part, 0.0, NEGATIVE)

    idx_keys = ik_all[...].reshape(keys, dim)
    w_rows = w_all[pl.ds(pl.multiple_of(h * part, part), part), :] * scale
    logits = jnp.zeros((part, keys), jnp.float32)
    group = 8
    for first in range(0, heads, group):
        stack = jnp.concatenate([iql[:, j * dim : (j + 1) * dim] for j in range(first, first + group)], axis=0)
        inner = lax.dot_general(stack, idx_keys, NT, preferred_element_type=jnp.float32)
        for j in range(group):
            gain = w_rows[:, first + j : first + j + 1]
            logits = logits + gain * jnp.maximum(inner[j * part : (j + 1) * part], 0.0)
        if first == 0:
            relay(lat_relays)
    logits = logits + bias_of(h)
    chance = jnp.exp(logits - jnp.max(logits, axis=-1, keepdims=True))
    chance = chance / jnp.sum(chance, axis=-1, keepdims=True)

    for copy in lat_arrivals:
        copy.wait_recv()
    for copy in q_loads:
        copy.wait()
    latents = lat_all[...].reshape(keys, width)
    blank = jnp.zeros((keys, shift), latents.dtype)
    k_even[...] = jnp.concatenate([latents, jnp.zeros((keys, key_width - width), latents.dtype)], axis=1)
    k_odd[...] = jnp.concatenate([jnp.zeros((keys, key_width - width), latents.dtype), latents], axis=1)

    step_pairs = math.gcd(pairs, 8)
    t_copies = []
    for k in range(1, hc + 1):
        chunk = others[k - 1] if k < hc else h
        bias = bias_of(chunk)

        def add_pairs(i, totals):
            q_rows = pl.ds(pl.multiple_of(chunk * part, part), part)
            q_pairs = pl.ds(i * step_pairs, step_pairs)
            for window, table in ((pl.ds(0, key_width), k_even), (pl.ds(shift, key_width), k_odd)):
                stack = q_buf[q_pairs, q_rows, window].reshape(step_pairs * part, key_width)
                scores = lax.dot_general(stack, table[...], NT, preferred_element_type=jnp.float32)
                scores = scores.reshape(step_pairs, part, keys) * (MAIN_SCALE * LOG2E) + bias[None]
                weights = jnp.exp2(scores - jnp.max(scores, axis=-1, keepdims=True))
                weights = weights * (1.0 / jnp.sum(weights, axis=-1, keepdims=True))
                totals = totals + jnp.sum(weights, axis=0)
            return totals

        totals = lax.fori_loop(0, pairs // step_pairs, add_pairs, jnp.zeros((part, keys), jnp.float32))
        if k < hc:
            t_send[k] = totals.astype(t_send.dtype)
            copy = pltpu.make_async_remote_copy(
                src_ref=t_send.at[k], dst_ref=t_recv.at[k], send_sem=t_s.at[k], recv_sem=t_r.at[k],
                device_id={"head": chunk}, device_id_type=MESH,
            )
            copy.start()
            t_copies.append(copy)
    for k in range(1, hc):
        t_copies[k - 1].wait_recv()
        totals = totals + t_recv[k].astype(jnp.float32)

    lane = lax.broadcasted_iota(jnp.int32, (part, rows), 1)
    line = lax.broadcasted_iota(jnp.int32, (part, rows), 0)
    cot = jnp.sum(jnp.where(lane == line + h * part, cot_ref[...], 0.0), axis=1, keepdims=True)
    upstream = (cot * (chance - totals * (1.0 / (2 * pairs * hc)))).astype(u_send.dtype)
    u_send[...] = upstream
    u_copies = []
    for k in range(1, hc):
        copy = pltpu.make_async_remote_copy(
            src_ref=u_send, dst_ref=u_all.at[h], send_sem=u_s.at[k], recv_sem=u_r.at[k],
            device_id={"head": others[k - 1]}, device_id_type=MESH,
        )
        copy.start()
        u_copies.append(copy)
    u_all[h] = upstream

    def stack_of(chunk):
        q_rows = pl.ds(pl.multiple_of(chunk * part, part), part)
        up = u_all[chunk].astype(jnp.float32)
        pieces = [iqg[q_rows, j * dim : (j + 1) * dim] for j in range(own_heads)]
        return q_rows, up, gains_all[q_rows, :], pieces, jnp.concatenate(pieces, axis=0)

    def add_key_grad(chunk, start):
        q_rows, up, gains, pieces, stack = stack_of(chunk)
        scaled = jnp.concatenate(
            [(pieces[j].astype(jnp.float32) * gains[:, j : j + 1]).astype(jnp.bfloat16) for j in range(own_heads)], axis=0
        )
        repeat = max(1, 128 // part)
        up_t = jnp.transpose(jnp.concatenate([up] * repeat, axis=0))
        up_wide = jnp.concatenate([up_t] * (own_heads // repeat), axis=1)
        inner_t = lax.dot_general(idx_keys, stack, NT, preferred_element_type=jnp.float32)
        grad_t = jnp.where(inner_t > 0.0, up_wide, 0.0).astype(jnp.bfloat16)
        term = jnp.dot(grad_t, scaled, preferred_element_type=jnp.float32)
        if start:
            dk[...] = term
        else:
            dk[...] += term

    column = lax.broadcasted_iota(jnp.int32, (part, gw_wide.shape[1]), 1)

    def put_query_grad(chunk):
        q_rows, up, gains, pieces, stack = stack_of(chunk)
        inner = lax.dot_general(stack, idx_keys, NT, preferred_element_type=jnp.float32)
        grad = jnp.where(inner.reshape(own_heads, part, keys) > 0.0, up[None], 0.0).astype(jnp.bfloat16)
        term = jnp.dot(grad.reshape(own_heads * part, keys), idx_keys, preferred_element_type=jnp.float32) * scale
        weight_grad = jnp.zeros((part, gw_wide.shape[1]), jnp.float32)
        for j in range(own_heads):
            own = term[j * part : (j + 1) * part]
            dot = jnp.sum(own * pieces[j].astype(jnp.float32), axis=1, keepdims=True)
            weight_grad = jnp.where(column == j, dot, weight_grad)
            gq_ref[q_rows, j * dim : (j + 1) * dim] = own * gains[:, j : j + 1]
        gw_wide[q_rows, :] = weight_grad

    add_key_grad(h, True)
    put_query_grad(h)
    for k in range(hc - 1, 0, -1):
        u_copies[k - 1].wait_recv()
        add_key_grad(sources[k - 1], False)
        if k == hc - 1:
            put_query_grad(sources[k - 1])
    dk_send[...] = (dk[...] * scale).astype(dk_send.dtype).reshape(n, block, dim)
    d_copies = []
    for t in range(1, n):
        peer = lax.rem(me + t, n)
        copy = pltpu.make_async_remote_copy(
            src_ref=dk_send.at[peer], dst_ref=dk_recv.at[t], send_sem=d_s.at[t], recv_sem=d_r.at[t],
            device_id={"ctx": peer}, device_id_type=MESH,
        )
        copy.start()
        d_copies.append(copy)
    for k in range(hc - 2, 0, -1):
        put_query_grad(sources[k - 1])
    gw_ref[...] = jnp.transpose(gw_wide[...])[:own_heads]

    own_block = dk[pl.ds(pl.multiple_of(me * block, block), block), :] * scale
    for t in range(1, n):
        d_copies[t - 1].wait_recv()
        own_block = own_block + dk_recv[t].astype(jnp.float32)
    z_send[...] = own_block.reshape(hc, block // hc, dim)
    z_copies = []
    for k in range(1, hc):
        peer = others[k - 1]
        copy = pltpu.make_async_remote_copy(
            src_ref=z_send.at[peer], dst_ref=z_recv.at[k], send_sem=z_s.at[k], recv_sem=z_r.at[k],
            device_id={"head": peer}, device_id_type=MESH,
        )
        copy.start()
        z_copies.append(copy)
    final = z_send[h]
    for k in range(1, hc):
        z_copies[k - 1].wait_recv()
        final = final + z_recv[k]
    gk_ref[...] = final

    relayed = [copy for step in ik_relays + lat_relays for copy in step]
    for copy in ik_direct + lat_direct + relayed + t_copies + u_copies + d_copies + z_copies:
        copy.wait_send()


def hand_out(gq_ref, gw_ref, gk_ref, gq_out, gw_out, gk_out):
    gq_out[...] = gq_ref[...]
    gw_out[...] = gw_ref[...]
    gk_out[...] = gk_ref[...]


def solution(mesh):
    n, hc = mesh.shape["ctx"], mesh.shape["head"]

    def step(main_query, latents, idx_query, idx_weight, idx_keys, kl_cotangent, query_start, key_start):
        rows, wide = main_query.shape
        block, width = latents.shape
        dim = idx_keys.shape[1]
        heads = idx_weight.shape[1]
        own_heads = heads // hc
        pairs = wide // (2 * width)
        keys = n * block
        key_width = pl.cdiv(width, 128) * 128
        part = rows // hc
        bf16, f32 = jnp.bfloat16, jnp.float32
        vmem = pl.BlockSpec(memory_space=pltpu.VMEM)
        smem = pl.BlockSpec(memory_space=pltpu.SMEM)
        hbm = pl.BlockSpec(memory_space=pl.ANY)
        dma = pltpu.SemaphoreType.DMA
        grads = pl.pallas_call(
            functools.partial(kernel, n, hc),
            out_shape=(
                jax.ShapeDtypeStruct((rows, heads * dim // hc), f32),
                jax.ShapeDtypeStruct((own_heads, rows), f32),
                jax.ShapeDtypeStruct((block // hc, dim), f32),
            ),
            in_specs=[smem, smem, hbm, vmem, hbm, vmem, vmem, vmem],
            out_specs=(vmem, vmem, vmem),
            scratch_shapes=[
                pltpu.VMEM((pairs, rows, 2 * width), bf16),
                pltpu.VMEM((part, heads * dim), bf16),
                pltpu.VMEM((rows, heads * dim // hc), bf16),
                pltpu.VMEM((n, block, width), bf16),
                pltpu.VMEM((n, block, dim), bf16),
                pltpu.VMEM((keys, key_width), bf16),
                pltpu.VMEM((keys, key_width), bf16),
                pltpu.VMEM((hc, part, keys), bf16),
                pltpu.VMEM((hc, part, keys), bf16),
                pltpu.VMEM((part, keys), bf16),
                pltpu.VMEM((hc, part, keys), bf16),
                pltpu.VMEM((rows, heads), f32),
                pltpu.VMEM((rows, heads // hc), f32),
                pltpu.VMEM((rows, 128), f32),
                pltpu.VMEM((keys, dim), f32),
                pltpu.VMEM((n, block, dim), bf16),
                pltpu.VMEM((n, block, dim), bf16),
                pltpu.VMEM((hc, block // hc, dim), f32),
                pltpu.VMEM((hc, block // hc, dim), f32),
                dma((pairs,)), dma((2,)),
                dma((n,)), dma((n,)), dma((n,)),
                dma((n,)), dma((n,)), dma((n,)),
                dma((hc,)), dma((hc,)), dma((hc,)), dma((hc,)),
                dma((n,)), dma((n,)), dma((hc,)), dma((hc,)),
            ],
            compiler_params=pltpu.CompilerParams(
                collective_id=0, has_side_effects=True, vmem_limit_bytes=60 * 2**20
            ),
        )(query_start, key_start, main_query, latents, idx_query, idx_weight.T, idx_keys, kl_cotangent.reshape(1, rows))
        strips = math.gcd(own_heads, 4)
        strip = own_heads // strips * dim
        by_strip = pl.BlockSpec((rows, strip), lambda i: (0, i))
        whole = [pl.BlockSpec(grad.shape, lambda i: (0, 0)) for grad in grads[1:]]
        grad_query, grad_weight, grad_keys = pl.pallas_call(
            hand_out,
            grid=(strips,),
            out_shape=tuple(jax.ShapeDtypeStruct(grad.shape, f32) for grad in grads),
            in_specs=[by_strip] + whole,
            out_specs=tuple([by_strip] + whole),
        )(*grads)
        return grad_query, grad_weight.T, grad_keys

    return jax.shard_map(
        step,
        mesh=mesh,
        in_specs=(
            P("ctx", "head"), P("ctx", None), P("ctx", None), P("ctx", None), P("ctx", None), P("ctx"), P(), P(),
        ),
        out_specs=(P("ctx", "head"), P("ctx", "head"), P(("ctx", "head"), None)),
        check_vma=False,
    )
```

time: 258 us -> 45 us (0.17)
  waiting for transfers between devices: 115 us -> 0 us
  Pallas kernels: 0 us -> 42.9 us
  blocking collectives: 39.5 us -> 0 us
  local copies, waits for them, and re-layouts: 37.3 us -> 0 us
  matrix products: 36.8 us -> 0 us
  between operations: 15.3 us -> 1.93 us
  other arithmetic: 13.1 us -> 0 us
    reduce_scatter x3 -> x0, waiting for transfers between devices: 94.4 us -> none  [the longest x1 77.7 us: shards(): lax.psum_scatter(query_grad.reshape(query_rows, idx_heads * idx_dim), 'he...]
    pallas_call x0 -> x2, Pallas kernels: none -> 42.9 us  [the longest x1 39.5 us: step(): pl.pallas_call(functools.partial(kernel, n, hc), out_shape=(jax.ShapeDtyp...]
    all_gather x4 -> x0, blocking collectives: 39.5 us -> none  [the longest x2 18.7 us: merged(): pieces = jax.tree.map(lambda part: lax.all_gather(part, axis), value)]
    unnamed x5 -> x0, waiting for transfers between devices: 20.8 us -> none
    div x4 -> x0, matrix products: 16.8 us -> none  [add_group(): weights = weights / jnp.sum(weights, axis=-1, keepdims=True)]
    sub x4 -> x0, matrix products: 14.3 us -> none  [add_group(): weights = jnp.where(visible[:, None, :], jnp.exp(scores - largest), 0.0)]
    unnamed x18 -> x0, local copies, waits for them, and re-layouts: 11.7 us -> none
    reshape x3 -> x0, local copies, waits for them, and re-layouts: 8.57 us -> none  [the longest x1 5.64 us: shards(): query_grad.reshape(query_rows, idx_heads * idx_dim)]
  transfers between devices with their start and end apart: 4 -> 0, of which waited for: 3 -> 0; matrix products, arithmetic and copies ran while one was open for 12% -> 0% of each run, Pallas kernels for 0% -> 0%
where the time goes in v1:
time: 45 us; the launch traced here: 44.8 us
  Pallas kernels  42.9 us (95%)
  between operations  1.93 us (4%)
    pallas_call x1, Pallas kernels, step(): pl.pallas_call(functools.partial(kernel, n, hc), out_shape=(jax.ShapeDtyp...  39.5 us
    pallas_call x1, Pallas kernels, step(): pl.pallas_call(hand_out, grid=(strips,), out_shape=tuple((jax.ShapeDtypeS...  3.38 us

profile of v1, /device:TPU:0, one launch (start us, length us, event | category | flops | bytes accessed | tf_op | source)
XLA Modules:
  0.0 44.8 jit_solution(11463809602139998194)
XLA Ops:
  1.9 39.5 %shard_map.103 = (f32[128,2048]{1,0:T(8,128)}, f32[16,128]{1,0:T(8,128)}, f32[16,128]{1,0:T(8,128)}) custom-call(s32[1]{0:T(128)S(6)} %copy.11.qs_ref, s32[1]{0:T(128)S(6)} %copy.12.ks_ref, bf16[128,18432]{1,0:T(8,128)(2,1)} %main_ref.1, bf16[64,576]{1,0:T(8,128)(2,1)} %lat_ref.1, bf16[128,8192]{1,0:T(8,128)(2,1)} %iq_ref.1, f32[64,128]{1,0:T(8,128)} %bitcast.3, ...), custom_call_target="tpu_custom_call" | custom-call | tf_op jit(solution)/shard_map/pallas_call | solution.py:303
  41.4 3.4 %shard_map.104 = (f32[128,2048]{1,0:T(8,128)}, f32[16,128]{1,0:T(8,128)}, f32[16,128]{1,0:T(8,128)}) custom-call(f32[128,2048]{1,0:T(8,128)} %get-tuple-element.9.gq_ref, f32[16,128]{1,0:T(8,128)} %get-tuple-element.10.gw_ref, f32[16,128]{1,0:T(8,128)} %get-tuple-element.11.gk_ref), custom_call_target="tpu_custom_call" | custom-call | tf_op jit(solution)/shard_map/pallas_call | solution.py:346

commit v2 on v1

--- a/solution.py
+++ b/solution.py
@@ -69,10 +69,10 @@
             device_id={"ctx": to}, device_id_type=MESH,
         )
 
-    def spread(src, dst, send, recv, forward):
+    def spread(src, dst, send, recv, forward, hops):
         direct, relays, arrivals = [], [], []
         own = push(src, dst, me, partner, forward.at[0], recv)
-        if n == 8:
+        if hops and n == 8:
             beside = me + 2 - 4 * lax.rem(me // 2, 2)
             across = me + 4 - 8 * (me // 4)
             far = beside + across - me
@@ -101,8 +101,8 @@
             for copy in step:
                 copy.start()
 
-    ik_direct, ik_relays, ik_arrivals = spread(ik_ref, ik_all, ik_s, ik_r, ik_f)
-    lat_direct, lat_relays, lat_arrivals = spread(lat_ref, lat_all, lat_s, lat_r, lat_f)
+    ik_direct, ik_relays, ik_arrivals = spread(ik_ref, ik_all, ik_s, ik_r, ik_f, False)
+    lat_direct, lat_relays, lat_arrivals = spread(lat_ref, lat_all, lat_s, lat_r, lat_f, True)
     for copy in ik_direct + lat_direct:
         copy.start()
     ik_all[me] = ik_ref[...]
@@ -111,6 +111,7 @@
     w_all[...] = w_t
     gains_all[...] = jnp.transpose(w_ref[pl.ds(pl.multiple_of(h * own_heads, own_heads), own_heads), :])
     relay(ik_relays)
+    relay(lat_relays[:-1])
     for copy in ik_arrivals:
         copy.wait_recv()
     for copy in loads:
@@ -132,22 +133,28 @@
         for j in range(group):
             gain = w_rows[:, first + j : first + j + 1]
             logits = logits + gain * jnp.maximum(inner[j * part : (j + 1) * part], 0.0)
-        if first == 0:
-            relay(lat_relays)
     logits = logits + bias_of(h)
     chance = jnp.exp(logits - jnp.max(logits, axis=-1, keepdims=True))
     chance = chance / jnp.sum(chance, axis=-1, keepdims=True)
 
-    for copy in lat_arrivals:
-        copy.wait_recv()
+    relay(lat_relays[-1:])
+    blank = jnp.zeros((block, key_width - width), lat_ref.dtype)
+
+    def place(at):
+        at_rows = pl.ds(pl.multiple_of(at * block, block), block)
+        latent = lat_all[at]
+        k_even[at_rows, :] = jnp.concatenate([latent, blank], axis=1)
+        k_odd[at_rows, :] = jnp.concatenate([blank, latent], axis=1)
+
+    for t in range(n // 2):
+        place(lax.rem(me + 2 * t, n))
+    for t in range(n // 2):
+        lat_arrivals[t].wait_recv()
+        place(lax.rem(partner - 2 * t + n, n))
     for copy in q_loads:
         copy.wait()
-    latents = lat_all[...].reshape(keys, width)
-    blank = jnp.zeros((keys, shift), latents.dtype)
-    k_even[...] = jnp.concatenate([latents, jnp.zeros((keys, key_width - width), latents.dtype)], axis=1)
-    k_odd[...] = jnp.concatenate([jnp.zeros((keys, key_width - width), latents.dtype), latents], axis=1)
-
-    step_pairs = math.gcd(pairs, 8)
+
+    step_pairs = math.gcd(pairs, 16)
     t_copies = []
     for k in range(1, hc + 1):
         chunk = others[k - 1] if k < hc else h
@@ -339,7 +346,7 @@
                 collective_id=0, has_side_effects=True, vmem_limit_bytes=60 * 2**20
             ),
         )(query_start, key_start, main_query, latents, idx_query, idx_weight.T, idx_keys, kl_cotangent.reshape(1, rows))
-        strips = math.gcd(own_heads, 4)
+        strips = 1
         strip = own_heads // strips * dim
         by_strip = pl.BlockSpec((rows, strip), lambda i: (0, i))
         whole = [pl.BlockSpec(grad.shape, lambda i: (0, 0)) for grad in grads[1:]]

time: 45 us -> 40.9 us (0.909)
  Pallas kernels: 42.9 us -> 38.8 us
    pallas_call x1, Pallas kernels: 39.5 us -> 36.5 us  [step(): pl.pallas_call(functools.partial(kernel, n, hc), out_shape=(jax.ShapeDtyp...]
    pallas_call x1, Pallas kernels: 3.38 us -> 2.29 us  [step(): pl.pallas_call(hand_out, grid=(strips,), out_shape=tuple((jax.ShapeDtypeS...]
where the time goes in v2:
time: 40.9 us; the launch traced here: 40.7 us
  Pallas kernels  38.8 us (95%)
  between operations  1.93 us (5%)
    pallas_call x1, Pallas kernels, step(): pl.pallas_call(functools.partial(kernel, n, hc), out_shape=(jax.ShapeDtyp...  36.5 us
    pallas_call x1, Pallas kernels, step(): pl.pallas_call(hand_out, grid=(strips,), out_shape=tuple((jax.ShapeDtypeS...  2.29 us

profile of v2, /device:TPU:0, one launch (start us, length us, event | category | flops | bytes accessed | tf_op | source)
XLA Modules:
  0.0 40.7 jit_solution(1725462126185210861)
XLA Ops:
  1.9 36.5 %shard_map.103 = (f32[128,2048]{1,0:T(8,128)}, f32[16,128]{1,0:T(8,128)}, f32[16,128]{1,0:T(8,128)}) custom-call(s32[1]{0:T(128)S(6)} %copy.11.qs_ref, s32[1]{0:T(128)S(6)} %copy.12.ks_ref, bf16[128,18432]{1,0:T(8,128)(2,1)} %main_ref.1, bf16[64,576]{1,0:T(8,128)(2,1)} %lat_ref.1, bf16[128,8192]{1,0:T(8,128)(2,1)} %iq_ref.1, f32[64,128]{1,0:T(8,128)} %bitcast.3, ...), custom_call_target="tpu_custom_call" | custom-call | tf_op jit(solution)/shard_map/pallas_call | solution.py:310
  38.4 2.3 %shard_map.104 = (f32[128,2048]{1,0:T(8,128)}, f32[16,128]{1,0:T(8,128)}, f32[16,128]{1,0:T(8,128)}) custom-call(f32[128,2048]{1,0:T(8,128)} %get-tuple-element.9.gq_ref, f32[16,128]{1,0:T(8,128)} %get-tuple-element.10.gw_ref, f32[16,128]{1,0:T(8,128)} %get-tuple-element.11.gk_ref), custom_call_target="tpu_custom_call" | custom-call | tf_op jit(solution)/shard_map/pallas_call | solution.py:353
